TPU v7x, 512 devices: a whole 4x8x8 slice. The times are simulated.
512 devices in a mesh: batch: 32 (over y_lo, z), seq: 16 (over y_hi, x, core).
Axes of the slice: x: 4, y: 8 (y_hi: 2, y_lo: 4; y = y_hi * 4 + y_lo), z: 8, core: 2. Of those that a mesh axis runs over, the one named last changes fastest.
Arguments:
- sequence_input: bfloat16 [32, 4096, 768], P('batch', 'seq'), may hold values from -64 to 64
- bn_gain: float32 [768], replicated, may hold values from 0.1 to 1.9
- bn_bias: float32 [768], replicated, may hold values from -3 to 3
- conv_weight: bfloat16 [5, 768, 768], P(None, None, 'batch'), may hold values from -0.09375 to 0.09375
- conv_bias: float32 [768], replicated, may hold values from -3 to 3
- ln_gain: float32 [768], replicated, may hold values from 0.1 to 1.9
- ln_bias: float32 [768], replicated, may hold values from -3 to 3
- qkv_weight: bfloat16 [768, 1792], P(None, 'batch'), may hold values from -32 to 32
Outputs:
- pooled: bfloat16 [32, 2048, 768], P('batch', 'seq')
- attended: bfloat16 [32, 2048, 768], P('batch', 'seq')
All inputs are finite; a program needn't handle non-finite values.
Results may differ from a plain program's by a relative error of at most 0.025.
The roundings to bfloat16 on the way count: a program that leaves them out, or rounds other values in their place, can miss the bound.
Values may be sent and summed in bfloat16 or wider, within the bound.
No kernel may reach another device: no remote copies, remote signals or barrier semaphores. Data moves between devices by JAX's collectives and lax.ppermute only.
A program may use at most 64 MiB of HBM per device.

v0:
```python
import jax
import jax.numpy as jnp
from jax import lax
from jax.sharding import PartitionSpec as P

HEADS = 8
KEY = 64
VAL = 96
epsilon = 1e-05


def extended(cells, sides, width):
    for axis, dim in sides:
        count = lax.axis_size(axis)
        ends = count - 1
        head = lax.slice_in_dim(cells, 0, width, axis=dim)
        tail = lax.slice_in_dim(cells, cells.shape[dim] - width, cells.shape[dim], axis=dim)
        cells = jnp.concatenate(
            [
                lax.ppermute(tail, axis, [(i, (i + 1) % count) for i in range(ends)]),
                cells,
                lax.ppermute(head, axis, [((i + 1) % count, i) for i in range(ends)]),
            ],
            axis=dim,
        )
    return cells


def conv_taps(padded, kernel, positions):
    result = None
    for tap_index in range(kernel.shape[0]):
        window = padded[:, tap_index : tap_index + positions]
        product = jnp.einsum(
            "slc,co->slo", window, kernel[tap_index], preferred_element_type=jnp.float32
        )
        result = product if result is None else result + product
    return result


def online_step(carry, query_rows, key_block, value_block):
    best, weight_sum, accum = carry
    scores = jnp.einsum(
        "sqhk,sjhk->shqj", query_rows, key_block, preferred_element_type=jnp.float32
    )
    newest = jnp.maximum(best, jnp.max(scores, axis=-1))
    fade = jnp.exp(best - newest)
    weights = jnp.exp(scores - newest[..., None])
    weight_sum = weight_sum * fade + jnp.sum(weights, axis=-1)
    accum = accum * fade[..., None] + jnp.einsum(
        "shqj,sjhv->shqv",
        weights.astype(jnp.bfloat16),
        value_block,
        preferred_element_type=jnp.float32,
    )
    return (newest, weight_sum, accum)


def blocked_attend(carry, query_rows, key_piece, value_piece):
    rows = key_piece.shape[1]
    block = min(rows, 512)
    for first in range(0, rows, block):
        carry = online_step(
            carry,
            query_rows,
            key_piece[:, first : first + block],
            value_piece[:, first : first + block],
        )
    return carry


def empty_state(seqs_here, heads_here, rows):
    return (
        jnp.full((seqs_here, heads_here, rows), -jnp.inf, jnp.float32),
        jnp.zeros((seqs_here, heads_here, rows), jnp.float32),
        jnp.zeros((seqs_here, heads_here, rows, VAL), jnp.float32),
    )


def on_device(
    sequence_input, bn_gain, bn_bias, conv_weight, conv_bias, ln_gain, ln_bias, qkv_weight
):
    seqs_here = sequence_input.shape[0]
    positions = sequence_input.shape[1]
    channels = sequence_input.shape[2]
    values_in = sequence_input.astype(jnp.float32)
    total, squares = lax.psum(
        (jnp.sum(values_in, axis=(0, 1)), jnp.sum(values_in * values_in, axis=(0, 1))),
        ("batch", "seq"),
    )
    count = float(seqs_here * positions * lax.axis_size("batch") * lax.axis_size("seq"))
    mean = total / count
    var = squares / count - mean * mean
    activated = jax.nn.gelu(
        (values_in - mean) * lax.rsqrt(var + epsilon) * bn_gain + bn_bias, approximate=True
    ).astype(jnp.bfloat16)
    padded = extended(activated, (("seq", 1),), 2)
    conv_out = conv_taps(
        padded, lax.all_gather(conv_weight, "batch", axis=2, tiled=True), positions
    )
    conv_out = conv_out + conv_bias
    bins_here = positions // 2
    pooled = conv_out.reshape(seqs_here, bins_here, 2, channels).max(axis=2).astype(jnp.bfloat16)
    pooled_wide = pooled.astype(jnp.float32)
    centre = jnp.mean(pooled_wide, axis=-1, keepdims=True)
    spread = jnp.mean((pooled_wide - centre) ** 2, axis=-1, keepdims=True)
    normed = ((pooled_wide - centre) * lax.rsqrt(spread + epsilon) * ln_gain + ln_bias).astype(
        jnp.bfloat16
    )
    proj = jnp.einsum(
        "sbd,dk->sbk",
        normed,
        lax.all_gather(qkv_weight, "batch", axis=1, tiled=True),
        preferred_element_type=jnp.float32,
    )
    head_keys = HEADS * KEY
    queries = (proj[..., :head_keys] * KEY ** (-0.5)).astype(jnp.bfloat16)
    key_rows = proj[..., head_keys : 2 * head_keys].astype(jnp.bfloat16)
    value_rows = proj[..., 2 * head_keys :].astype(jnp.bfloat16)
    query_heads = queries.reshape(seqs_here, bins_here, HEADS, KEY)
    key_piece = lax.all_gather(key_rows, "seq", axis=1, tiled=True)
    value_piece = lax.all_gather(value_rows, "seq", axis=1, tiled=True)
    width_now = key_piece.shape[1]
    best, weight_sum, accum = blocked_attend(
        empty_state(seqs_here, HEADS, bins_here),
        query_heads,
        key_piece.reshape(seqs_here, width_now, HEADS, KEY),
        value_piece.reshape(seqs_here, width_now, HEADS, VAL),
    )
    attended = (
        (accum / weight_sum[..., None])
        .transpose(0, 2, 1, 3)
        .reshape(seqs_here, bins_here, HEADS * VAL)
        .astype(jnp.bfloat16)
    )
    return (pooled, attended)


def solution(mesh):
    placed = (
        P("batch", "seq", None),
        P(),
        P(),
        P(None, None, "batch"),
        P(),
        P(),
        P(),
        P(None, "batch"),
    )
    return jax.shard_map(
        on_device,
        mesh=mesh,
        in_specs=placed,
        out_specs=(P("batch", "seq", None), P("batch", "seq", None)),
        check_vma=False,
    )
```

profile of v0, /device:TPU:1, one launch (start us, length us, event | category | flops | bytes accessed | tf_op | source)
XLA Modules:
  0.0 494.9 jit_solution(5999719984073595939)
XLA Ops:
  7.2 0.0 all-gather.5.cloned.1.call-start
  7.2 0.7 all-gather.5.cloned.1.call-update
  7.9 0.0 all-gather.7.cloned.1.call-start
  7.9 0.7 all-gather.7.cloned.1.call-update
  8.6 0.0 all-gather.9.cloned.1.call-start
  8.7 1.1 convert_reduce_fusion
  9.8 109.2 %all-reduce = (f32[768]{0:T(1024)S(1)}, f32[768]{0:T(1024)S(1)}) all-reduce(f32[768]{0:T(1024)S(1)} %get-tuple-element.7, f32[768]{0:T(1024)S(1)} %get-tuple-element.6), channel_id=1, replica_groups=mesh['batch'=32,'seq'=16] {'batch','seq'}, use_global_device_ids=true, to_apply=%region_3.0 | all-reduce | flops 1536 | bytes 12288 | tf_op jit(solution)/shard_map/psum | solution.py:86
  119.0 1.4 fusion.28
  120.5 5.3 %collective-permute-start = (bf16[1,2,768]{2,1,0:T(2,128)(2,1)S(1)}, bf16[1,2,768]{2,1,0:T(2,128)(2,1)S(1)}, u32[]{:S(2)}, u32[]{:S(2)}) collective-permute-start(bf16[1,2,768]{2,1,0:T(2,128)(2,1)S(1)} %get-tuple-element.18), channel_id=1, source_target_pairs={{0,1},{1,2},{2,3},{3,4},{4,5},{5,6},{6,7},{7,8},{8,9},{9,10},{10,1... | collective-permute-start | bytes 9224 | tf_op jit(solution)/shard_map/ppermute | solution.py:20
  125.8 1.9 collective-permute-start.1
  127.7 0.0 collective-permute-done
  127.7 33.8 %all-gather.5.cloned.1.call-done = bf16[5,768,768]{1,2,0:T(8,128)(2,1)} async-done(((bf16[5,768,24]{1,2,0:T(8,128)(2,1)}), bf16[5,768,768]{1,2,0:T(8,128)(2,1)}) %all-gather.5.cloned.1.call-update) | async-done | bytes 5898256 | tf_op jit(solution)/shard_map/all_gather | solution.py:98
  161.5 1.9 fusion.13
  163.4 1.9 convolution_add_fusion.3
  165.4 0.0 copy-done.9
  165.4 0.5 convolution_add_fusion.2
  165.9 0.0 copy-start.12
  165.9 0.0 collective-permute-done.1
  165.9 0.5 convolution_add_fusion.1
  166.4 0.1 copy-done.12
  166.6 0.5 fusion.8
  167.1 0.1 reshape.416
  167.3 1.0 reduce_max.45
  168.3 0.0 copy-start.8
  168.3 0.1 convert_reduce_fusion.1
  168.4 0.2 multiply_reduce_fusion
  168.6 146.7 %all-gather.7.cloned.1.call-done = bf16[768,1792]{0,1:T(8,128)(2,1)} async-done(((bf16[768,56]{0,1:T(8,128)(2,1)}), bf16[768,1792]{0,1:T(8,128)(2,1)}) %all-gather.7.cloned.1.call-update) | async-done | bytes 2752528 | tf_op jit(solution)/shard_map/all_gather | solution.py:112
  315.3 0.0 copy-done.10
  315.3 0.0 copy-done.11
  315.3 2.8 fusion.69
  318.1 0.0 copy-done.8
  318.2 0.6 slice.106
  318.8 0.0 all-gather.9.cloned.1.call-update
  318.8 0.2 all-gather.11.cloned.1.call-start
  319.1 0.7 slice.108
  319.7 0.0 all-gather.11.cloned.1.call-update
  319.8 0.1 copy.23
  319.9 81.3 %all-gather.9.cloned.1.call-done = bf16[1,2048,512]{2,1,0:T(8,128)(2,1)} async-done(((bf16[1,128,512]{2,1,0:T(8,128)(2,1)}), bf16[1,2048,512]{2,1,0:T(8,128)(2,1)}) %all-gather.9.cloned.1.call-update) | async-done | bytes 2097168 | tf_op jit(solution)/shard_map/all_gather | solution.py:120
  401.3 2.9 copy.24
  404.2 0.0 copy-start.6
  404.2 1.4 copy-done.6
  405.6 0.6 fusion.71
  406.1 0.0 copy-start.7
  406.1 2.2 fusion.72
  408.3 0.3 copy-done.7
  408.6 0.6 fusion.73
  409.2 0.6 fusion.70
  409.8 0.0 copy-done.4
  409.8 1.2 fusion
  411.0 0.2 copy-done.2
  411.2 0.0 copy-done
  411.2 1.2 fusion.2
  412.4 63.9 %all-gather.11.cloned.1.call-done = bf16[1,2048,768]{2,1,0:T(8,128)(2,1)} async-done(((bf16[1,128,768]{2,1,0:T(8,128)(2,1)}), bf16[1,2048,768]{2,1,0:T(8,128)(2,1)}) %all-gather.11.cloned.1.call-update) | async-done | bytes 3145744 | tf_op jit(solution)/shard_map/all_gather | solution.py:121
  476.3 4.7 copy.25
  481.0 2.5 fusion.12
  483.4 0.0 copy-start.3
  483.4 0.0 copy-done.1
  483.5 1.8 fusion.11
  485.3 0.0 copy-start.5
  485.3 0.3 copy-done.3
  485.6 0.6 fusion.10
  486.2 0.8 copy-done.5
  487.0 0.6 fusion.14
  487.6 0.8 copy.26
  (14 shorter events, 0.1 us)
Async XLA Ops:
  7.2 154.3 %all-gather.5.cloned.1.call-start = ((), (), s32[]{:S(2)}) async-start(), calls=%async_computation | async-start | bytes 6082560 | tf_op jit(solution)/shard_map/all_gather | solution.py:98
  7.9 307.4 %all-gather.7.cloned.1.call-start = ((), (), s32[]{:S(2)}) async-start(), calls=%async_computation.1 | async-start | bytes 2838528 | tf_op jit(solution)/shard_map/all_gather | solution.py:112
  8.6 392.6 %all-gather.9.cloned.1.call-start = ((), (), s32[]{:S(2)}) async-start(), calls=%async_computation.2 | async-start | bytes 2228224 | tf_op jit(solution)/shard_map/all_gather | solution.py:120
  120.5 7.3 %collective-permute-start = (bf16[1,2,768]{2,1,0:T(2,128)(2,1)S(1)}, bf16[1,2,768]{2,1,0:T(2,128)(2,1)S(1)}, u32[]{:S(2)}, u32[]{:S(2)}) collective-permute-start(bf16[1,2,768]{2,1,0:T(2,128)(2,1)S(1)} %get-tuple-element.18), channel_id=1, source_target_pairs={{0,1},{1,2},{2,3},{3,4},{4,5},{5,6},{6,7},{7,8},{8,9},{9,10},{10,1... | collective-permute-start | bytes 9224 | tf_op jit(solution)/shard_map/ppermute | solution.py:20
  125.8 40.1 %collective-permute-start.1 = (bf16[1,2,768]{2,1,0:T(2,128)(2,1)S(1)}, bf16[1,2,768]{2,1,0:T(2,128)(2,1)S(1)}, u32[]{:S(2)}, u32[]{:S(2)}) collective-permute-start(bf16[1,2,768]{2,1,0:T(2,128)(2,1)S(1)} %get-tuple-element.17), channel_id=1, source_target_pairs={{1,0},{2,1},{3,2},{4,3},{5,4},{6,5},{7,6},{8,7},{9,8},{10,9},{11,1... | collective-permute-start | bytes 9224 | tf_op jit(solution)/shard_map/ppermute | solution.py:22
  161.5 3.9 copy-start.9
  165.9 0.7 copy-start.12
  166.6 148.7 %copy-start.10 = (f32[768]{0:T(1024)S(1)}, f32[768]{0:T(1024)}, u32[]{:S(2)}) copy-start(f32[768]{0:T(1024)} %param.14) | copy-start | bytes 9220
  166.6 148.7 %copy-start.11 = (f32[768]{0:T(1024)S(1)}, f32[768]{0:T(1024)}, u32[]{:S(2)}) copy-start(f32[768]{0:T(1024)} %param.13) | copy-start | bytes 9220
  168.3 149.8 %copy-start.8 = (bf16[128,768]{1,0:T(8,128)(2,1)}, bf16[128,768]{1,0:T(8,128)(2,1)S(1)}, u32[]{:S(2)}) copy-start(bf16[128,768]{1,0:T(8,128)(2,1)S(1)} %reduce_max.45) | copy-start | bytes 589828
  318.8 157.4 %all-gather.11.cloned.1.call-start = ((), (), s32[]{:S(2)}) async-start(), calls=%async_computation.3 | async-start | bytes 3342336 | tf_op jit(solution)/shard_map/all_gather | solution.py:121
  404.2 1.4 copy-start.6
  406.1 3.7 copy-start.4
  406.1 2.5 copy-start.7
  409.2 2.0 copy-start
  409.8 1.4 copy-start.2
  481.0 2.5 copy-start.1
  483.4 2.1 copy-start.3
  485.3 1.7 copy-start.5
Sparse Core Ops, SparseCore 0:
  10.1 151.3 all-gather.4
  163.6 151.6 all-gather.6
  318.9 82.2 all-gather.8
  405.0 71.1 all-gather.10
where the time goes:
time: 495 us
  waiting for transfers between devices  327 us (66%)
  blocking collectives  109 us (22%)
  matrix products  17.5 us (4%)
  between operations  14 us (3%)
  local copies, waits for them, and re-layouts  13.2 us (3%)
  starting transfers between devices  7.58 us (2%)
  other arithmetic  6.26 us (1%)
    all_gather x1, waiting for transfers between devices, on_device(): lax.all_gather(qkv_weight, 'batch', axis=1, tiled=True)  147 us
    psum x1, blocking collectives, on_device(): lax.psum((jnp.sum(values_in, axis=(0, 1)), jnp.sum(values_in * values_in,...  109 us
    all_gather x1, waiting for transfers between devices, on_device(): key_piece = lax.all_gather(key_rows, 'seq', axis=1, tiled=True)  81.3 us
    all_gather x1, waiting for transfers between devices, on_device(): value_piece = lax.all_gather(value_rows, 'seq', axis=1, tiled=True)  63.9 us
    all_gather x1, waiting for transfers between devices, on_device(): lax.all_gather(conv_weight, 'batch', axis=2, tiled=True)  33.8 us
  transfers between devices with their start and end apart: 6, of which 4 were waited for; matrix products, arithmetic and copies ran while one was open for 4% of the time, Pallas kernels for 0%

commit v1 on v0

--- a/solution.py
+++ b/solution.py
@@ -118,7 +118,9 @@
     value_rows = proj[..., 2 * head_keys :].astype(jnp.bfloat16)
     query_heads = queries.reshape(seqs_here, bins_here, HEADS, KEY)
     key_piece = lax.all_gather(key_rows, "seq", axis=1, tiled=True)
-    value_piece = lax.all_gather(value_rows, "seq", axis=1, tiled=True)
+    value_piece = jnp.concatenate(
+        lax.all_to_all(jnp.stack([value_rows] * lax.axis_size("seq")), "seq", 0, 0), axis=1
+    )
     width_now = key_piece.shape[1]
     best, weight_sum, accum = blocked_attend(
         empty_state(seqs_here, HEADS, bins_here),

time: 495 us -> 477 us (0.964)
  the two profiles are of different devices: /device:TPU:1 before, /device:TPU:25 now
where the time goes in v1:
time: 477 us; the launch traced here: 476 us
  waiting for transfers between devices  272 us (57%)
  blocking collectives  109 us (23%)
  starting transfers between devices  35.5 us (7%)
  local copies, waits for them, and re-layouts  20.7 us (4%)
  matrix products  18.5 us (4%)
  between operations  14 us (3%)
  other arithmetic  6.27 us (1%)
    all_gather x1, waiting for transfers between devices, on_device(): lax.all_gather(qkv_weight, 'batch', axis=1, tiled=True)  147 us
    psum x1, blocking collectives, on_device(): lax.psum((jnp.sum(values_in, axis=(0, 1)), jnp.sum(values_in * values_in,...  109 us
    all_gather x1, waiting for transfers between devices, on_device(): key_piece = lax.all_gather(key_rows, 'seq', axis=1, tiled=True)  101 us
    all_to_all x1, starting transfers between devices, on_device(): lax.all_to_all(jnp.stack([value_rows] * lax.axis_size('seq')), 'seq', 0, 0)  28.3 us
    all_gather x1, waiting for transfers between devices, on_device(): lax.all_gather(conv_weight, 'batch', axis=2, tiled=True)  23.5 us
  transfers between devices with their start and end apart: 6, of which 3 were waited for; matrix products, arithmetic and copies ran while one was open for 5% of the time, Pallas kernels for 0%

profile of v1, /device:TPU:25, one launch (start us, length us, event | category | flops | bytes accessed | tf_op | source)
XLA Modules:
  0.0 476.4 jit_solution(3661006029860878029)
XLA Ops:
  7.2 0.0 all-gather.4.cloned.1.call-start
  7.2 0.7 all-gather.4.cloned.1.call-update
  7.9 0.0 all-gather.6.cloned.1.call-start
  7.9 0.7 all-gather.6.cloned.1.call-update
  8.6 0.0 all-gather.8.cloned.1.call-start
  8.7 1.1 convert_reduce_fusion
  9.8 109.0 %all-reduce = (f32[768]{0:T(1024)S(1)}, f32[768]{0:T(1024)S(1)}) all-reduce(f32[768]{0:T(1024)S(1)} %get-tuple-element.9, f32[768]{0:T(1024)S(1)} %get-tuple-element.8), channel_id=1, replica_groups=mesh['batch'=32,'seq'=16] {'batch','seq'}, use_global_device_ids=true, to_apply=%region_3.0 | all-reduce | flops 1536 | bytes 12288 | tf_op jit(solution)/shard_map/psum | solution.py:86
  118.8 1.4 fusion.28
  120.2 5.2 %collective-permute-start = (bf16[1,2,768]{2,1,0:T(2,128)(2,1)S(1)}, bf16[1,2,768]{2,1,0:T(2,128)(2,1)S(1)}, u32[]{:S(2)}, u32[]{:S(2)}) collective-permute-start(bf16[1,2,768]{2,1,0:T(2,128)(2,1)S(1)} %get-tuple-element.20), channel_id=1, source_target_pairs={{0,1},{1,2},{2,3},{3,4},{4,5},{5,6},{6,7},{7,8},{8,9},{9,10},{10,1... | collective-permute-start | bytes 9224 | tf_op jit(solution)/shard_map/ppermute | solution.py:20
  125.4 1.9 collective-permute-start.1
  127.3 0.0 collective-permute-done
  127.4 23.5 %all-gather.4.cloned.1.call-done = bf16[5,768,768]{1,2,0:T(8,128)(2,1)} async-done(((bf16[5,768,24]{1,2,0:T(8,128)(2,1)}), bf16[5,768,768]{1,2,0:T(8,128)(2,1)}) %all-gather.4.cloned.1.call-update) | async-done | bytes 5898256 | tf_op jit(solution)/shard_map/all_gather | solution.py:98
  150.8 0.0 copy-start.8
  150.8 1.9 fusion.13
  152.8 1.9 convolution_add_fusion.3
  154.7 0.0 copy-done.8
  154.7 0.5 convolution_add_fusion.2
  155.2 0.0 copy-start.11
  155.2 0.0 collective-permute-done.1
  155.2 0.5 convolution_add_fusion.1
  155.8 0.1 copy-done.11
  155.9 0.0 copy-start.9
  155.9 0.5 fusion.8
  156.4 0.1 reshape.416
  156.6 1.0 reduce_max.45
  157.6 0.0 copy-start.7
  157.6 0.1 convert_reduce_fusion.1
  157.8 0.2 multiply_reduce_fusion
  158.0 147.0 %all-gather.6.cloned.1.call-done = bf16[768,1792]{0,1:T(8,128)(2,1)} async-done(((bf16[768,56]{0,1:T(8,128)(2,1)}), bf16[768,1792]{0,1:T(8,128)(2,1)}) %all-gather.6.cloned.1.call-update) | async-done | bytes 2752528 | tf_op jit(solution)/shard_map/all_gather | solution.py:112
  305.0 0.0 copy-done.9
  305.0 0.0 copy-done.10
  305.0 2.8 fusion.69
  307.9 0.0 copy-done.7
  307.9 0.7 slice.106
  308.5 0.0 all-gather.8.cloned.1.call-update
  308.6 0.2 copy.26
  308.7 2.3 stack.2
  311.1 28.3 %all-to-all-start = ((bf16[16,1,128,768]{2,3,1,0:T(8,128)(2,1)}), bf16[16,1,128,768]{2,3,1,0:T(8,128)(2,1)}, u32[]{:S(2)}, u32[]{:S(2)}) async-start(bf16[16,1,128,768]{2,3,1,0:T(8,128)(2,1)} %stack.2), calls=%async_computation | async-start | bytes 6291456 | tf_op jit(solution)/shard_map/all_to_all | solution.py:122
  339.4 0.1 copy.24
  339.5 100.6 %all-gather.8.cloned.1.call-done = bf16[1,2048,512]{2,1,0:T(8,128)(2,1)} async-done(((bf16[1,128,512]{2,1,0:T(8,128)(2,1)}), bf16[1,2048,512]{2,1,0:T(8,128)(2,1)}) %all-gather.8.cloned.1.call-update) | async-done | bytes 2097168 | tf_op jit(solution)/shard_map/all_gather | solution.py:120
  440.1 2.9 copy.25
  443.0 0.0 copy-start.6
  443.0 0.6 fusion.70
  443.6 0.7 copy-done.6
  444.3 0.6 fusion.71
  444.9 2.0 fusion.72
  446.9 1.6 fusion.73
  448.5 0.0 copy-done
  448.5 0.0 copy-done.4
  448.6 1.2 fusion
  449.7 0.1 copy-done.1
  449.8 1.2 fusion.2
  451.0 0.0 all-to-all-done
  451.0 5.6 %copy.27 = bf16[16,1,128,768]{2,0,3,1:T(8,128)(2,1)} copy(bf16[16,1,128,768]{2,3,1,0:T(8,128)(2,1)} %all-to-all-done) | data formatting | bytes 6291456 | tf_op jit(solution)/shard_map/all_to_all | solution.py:122
  456.6 5.8 %reshape_reshape.3 = bf16[1,2048,8,96]{1,3,2,0:T(8,128)(2,1)} reshape(bf16[16,1,128,768]{2,0,3,1:T(8,128)(2,1)} %copy.27) | data formatting | bytes 6291456 | tf_op jit(solution)/shard_map/reshape;reshape | solution.py:129
  462.4 2.5 fusion.12
  464.9 0.0 copy-start.3
  464.9 0.0 copy-done.2
  464.9 1.8 fusion.11
  466.8 0.3 copy-done.3
  467.1 0.6 fusion.10
  467.7 0.8 copy-done.5
  468.4 0.6 fusion.14
  469.0 0.8 copy.28
  (14 shorter events, 0.1 us)
Async XLA Ops:
  7.2 143.7 %all-gather.4.cloned.1.call-start = ((), (), s32[]{:S(2)}) async-start(), calls=%async_computation.1 | async-start | bytes 6082560 | tf_op jit(solution)/shard_map/all_gather | solution.py:98
  7.9 297.1 %all-gather.6.cloned.1.call-start = ((), (), s32[]{:S(2)}) async-start(), calls=%async_computation.2 | async-start | bytes 2838528 | tf_op jit(solution)/shard_map/all_gather | solution.py:112
  8.6 431.4 %all-gather.8.cloned.1.call-start = ((), (), s32[]{:S(2)}) async-start(), calls=%async_computation.3 | async-start | bytes 2228224 | tf_op jit(solution)/shard_map/all_gather | solution.py:120
  120.2 7.1 %collective-permute-start = (bf16[1,2,768]{2,1,0:T(2,128)(2,1)S(1)}, bf16[1,2,768]{2,1,0:T(2,128)(2,1)S(1)}, u32[]{:S(2)}, u32[]{:S(2)}) collective-permute-start(bf16[1,2,768]{2,1,0:T(2,128)(2,1)S(1)} %get-tuple-element.20), channel_id=1, source_target_pairs={{0,1},{1,2},{2,3},{3,4},{4,5},{5,6},{6,7},{7,8},{8,9},{9,10},{10,1... | collective-permute-start | bytes 9224 | tf_op jit(solution)/shard_map/ppermute | solution.py:20
  125.4 29.8 %collective-permute-start.1 = (bf16[1,2,768]{2,1,0:T(2,128)(2,1)S(1)}, bf16[1,2,768]{2,1,0:T(2,128)(2,1)S(1)}, u32[]{:S(2)}, u32[]{:S(2)}) collective-permute-start(bf16[1,2,768]{2,1,0:T(2,128)(2,1)S(1)} %get-tuple-element.19), channel_id=1, source_target_pairs={{1,0},{2,1},{3,2},{4,3},{5,4},{6,5},{7,6},{8,7},{9,8},{10,9},{11,1... | collective-permute-start | bytes 9224 | tf_op jit(solution)/shard_map/ppermute | solution.py:22
  150.8 3.9 copy-start.8
  155.2 0.7 copy-start.11
  155.9 149.1 %copy-start.9 = (f32[768]{0:T(1024)S(1)}, f32[768]{0:T(1024)}, u32[]{:S(2)}) copy-start(f32[768]{0:T(1024)} %param.14) | copy-start | bytes 9220
  155.9 149.1 %copy-start.10 = (f32[768]{0:T(1024)S(1)}, f32[768]{0:T(1024)}, u32[]{:S(2)}) copy-start(f32[768]{0:T(1024)} %param.13) | copy-start | bytes 9220
  157.6 150.2 %copy-start.7 = (bf16[128,768]{1,0:T(8,128)(2,1)}, bf16[128,768]{1,0:T(8,128)(2,1)S(1)}, u32[]{:S(2)}) copy-start(bf16[128,768]{1,0:T(8,128)(2,1)S(1)} %reduce_max.45) | copy-start | bytes 589828
  311.1 139.9 %all-to-all-start = ((bf16[16,1,128,768]{2,3,1,0:T(8,128)(2,1)}), bf16[16,1,128,768]{2,3,1,0:T(8,128)(2,1)}, u32[]{:S(2)}, u32[]{:S(2)}) async-start(bf16[16,1,128,768]{2,3,1,0:T(8,128)(2,1)} %stack.2), calls=%async_computation | async-start | bytes 6291456 | tf_op jit(solution)/shard_map/all_to_all | solution.py:122
  443.0 1.3 copy-start.6
  444.3 4.2 copy-start
  444.9 3.7 copy-start.4
  448.5 1.3 copy-start.1
  462.4 2.5 copy-start.2
  464.9 2.1 copy-start.3
  466.8 1.7 copy-start.5
Sparse Core Ops, SparseCore 0:
  10.1 140.6 all-gather.3
  152.9 152.0 all-gather.5
  308.9 131.1 all-gather.7
